TPU v7x, 128 devices: a whole 4x4x4 slice. The times are simulated.
128 devices in a mesh: walker: 32 (over x, z, core), owner: 4 (over y).
Axes of the slice: x: 4, y: 4, z: 4, core: 2. Of those that a mesh axis runs over, the one named last changes fastest.
Arguments:
- block_input_rows: bfloat16 [2048, 1024, 256], P(('walker', 'owner')), may hold values from -6 to 6
- spin_values: int32 [2048, 1024], P(('walker', 'owner')), may hold values 0 or 1
- conv_weight: bfloat16 [256, 512], replicated, may hold values from -0.25 to 0.25
- conv_bias: float32 [256], replicated, may hold values from -3 to 3
- readout: float32 [256], replicated, may hold values from -0.375 to 0.375
- energies: float32 [2048], P(('walker', 'owner')), may hold values from -1 to 0.1
- basis_out: bfloat16 [256, 256], P(None, 'owner'), may hold values from -0.375 to 0.375
- basis_in: bfloat16 [512, 512], P(None, 'owner'), may hold values from -6 to 6
Outputs:
- moment_stats: float32 [256, 512], P(None, 'owner')
- update: float32 [256, 512], P(None, 'owner')
All inputs are finite; a program needn't handle non-finite values. No bound on the sum of `spin_values` on one device may be relied on, other than what follows from the above.
Results may differ from a plain program's by a relative error of at most 0.025.
Values may be sent and summed in bfloat16 or wider, within the bound.
A program may use at most 128 MiB of HBM per device.

v0:
```python
import jax
import jax.numpy as jnp
from jax import lax
from jax.sharding import PartitionSpec as P

DILATION_STEP = 16
DAMPING = 0.01


def body(
    block_input_rows, spin_values, conv_weight, conv_bias, readout, energies, basis_out, basis_in
):
    local_sample_count = block_input_rows.shape[0]
    chain_site_count = block_input_rows.shape[1]
    channel_count = block_input_rows.shape[2]
    total_samples = local_sample_count * lax.axis_size("walker") * lax.axis_size("owner")
    energy_total = lax.psum(jnp.sum(energies), ("walker", "owner"))
    energy_mean = energy_total / total_samples
    full_out = lax.all_gather(basis_out, "owner", axis=1, tiled=True)
    now_part = jnp.einsum(
        "slc,oc->slo",
        block_input_rows,
        conv_weight[:, channel_count:],
        preferred_element_type=jnp.float32,
    )
    earlier_portion = jnp.einsum(
        "slc,oc->slo",
        block_input_rows,
        conv_weight[:, :channel_count],
        preferred_element_type=jnp.float32,
    )
    delayed_input = jnp.concatenate(
        [
            jnp.zeros((local_sample_count, DILATION_STEP, channel_count), jnp.float32),
            earlier_portion[:, : chain_site_count - DILATION_STEP],
        ],
        axis=1,
    )
    pre_act = now_part + delayed_input + conv_bias
    activation = jnp.tanh(pre_act)
    logit_rows = jnp.sum((block_input_rows.astype(jnp.float32) + activation) * readout, axis=-1)
    target = spin_values.astype(jnp.float32)
    backward_signal = (
        (0.5 * (target - jax.nn.sigmoid(logit_rows)))[:, :, None]
        * readout
        * (1.0 - activation * activation)
    )
    backward_signal = backward_signal.astype(jnp.bfloat16)
    grad_now = jnp.einsum(
        "slo,slc->soc", backward_signal, block_input_rows, preferred_element_type=jnp.float32
    )
    gradient_earlier = jnp.einsum(
        "slo,slc->soc",
        backward_signal[:, DILATION_STEP:],
        block_input_rows[:, : chain_site_count - DILATION_STEP],
        preferred_element_type=jnp.float32,
    )
    gradient = jnp.concatenate([gradient_earlier, grad_now], axis=2).astype(jnp.bfloat16)
    half_proj = jnp.einsum(
        "ok,soc->skc", full_out, gradient, preferred_element_type=jnp.float32
    ).astype(jnp.bfloat16)
    sample_weights = energies - energy_mean
    panel_width = basis_in.shape[1]
    projected = jnp.einsum(
        "skc,cm->skm",
        half_proj,
        lax.all_gather(basis_in, "owner", axis=1, tiled=True),
        preferred_element_type=jnp.float32,
    )
    squares = jnp.sum(projected * projected, axis=0)
    weighted = jnp.einsum("s,skm->km", sample_weights, projected)
    stacked = jnp.stack([squares, weighted], axis=0)
    totals = lax.psum(stacked, ("walker", "owner"))
    owner_panel = lax.dynamic_slice_in_dim(
        totals, lax.axis_index("owner") * panel_width, panel_width, 2
    )
    stats_part = owner_panel[0] / total_samples
    centered = owner_panel[1] / total_samples
    ratio_float = centered / (stats_part + DAMPING)
    scaled_ratio = ratio_float.astype(jnp.bfloat16)
    mixed_basis = jnp.dot(full_out, scaled_ratio, preferred_element_type=jnp.float32).astype(
        jnp.bfloat16
    )
    back_term = jnp.dot(mixed_basis, basis_in.T, preferred_element_type=jnp.float32)
    raw_update = lax.psum_scatter(back_term, "owner", scatter_dimension=1, tiled=True)
    square_total = lax.psum(jnp.sum(raw_update * raw_update), "owner")
    mean_sq = square_total / (channel_count * 2 * channel_count)
    return (stats_part, raw_update / jnp.sqrt(mean_sq + 1e-06))


def solution(mesh):
    in_specs = (
        P(("walker", "owner"), None, None),
        P(("walker", "owner"), None),
        P(),
        P(),
        P(),
        P(("walker", "owner")),
        P(None, "owner"),
        P(None, "owner"),
    )
    out_specs = (P(None, "owner"), P(None, "owner"))
    return jax.shard_map(body, mesh=mesh, in_specs=in_specs, out_specs=out_specs, check_vma=False)
```

profile of v0, /device:TPU:0, one launch (start us, length us, event | category | flops | bytes accessed | tf_op | source)
XLA Modules:
  0.0 357.1 jit_solution(8199990316887416576)
XLA Ops:
  7.2 0.0 copy-start.2
  7.2 0.0 copy-start.6
  7.2 0.0 copy-start.5
  7.2 0.0 all-reduce.3.cloned.1.call-start
  7.2 11.4 %fusion.5 = f32[16,1008,256]{2,1,0:T(8,128)} fusion(bf16[16,1024,256]{2,1,0:T(8,128)(2,1)} %param.8, bf16[256,512]{1,0:T(8,128)(2,1)} %param.10), kind=kOutput, calls=%fused_computation.9 | convolution fusion | flops 2113929216 | bytes 24903680 | tf_op jit(solution)/shard_map/slc,oc->slo/dot_general | solution.py:26
  18.6 0.0 copy-done.2
  18.6 0.0 copy-done.6
  18.6 0.0 copy-done.5
  18.6 0.0 copy-start.3
  18.6 16.8 %multiply_reduce_fusion = (f32[16,1024]{1,0:T(8,128)S(1)}, f32[16,1024,256]{2,1,0:T(8,128)}) fusion(bf16[16,1024,256]{2,1,0:T(8,128)(2,1)} %param.8, f32[256]{0:T(256)S(1)} %copy-done.5, f32[256]{0:T(256)S(1)} %copy-done.6, f32[16,1008,256]{2,1,0:T(8,128)} %fusion.5, bf16[256,512]{1,0:T(8,128)(2,1)S(1)} %copy-done.2), kind=kOutput, calls=%fused_computation.1 | convolution fusion | flops 2172633088 | bytes 50268160 | tf_op jit(solution)/shard_map/slc,oc->slo/dot_general | solution.py:20
  35.5 0.0 copy-done.3
  35.5 10.0 %multiply_convert_fusion = bf16[16,1024,256]{2,1,0:T(8,128)(2,1)} fusion(f32[16,1024,256]{2,1,0:T(8,128)} %get-tuple-element.3, f32[16,1024]{1,0:T(8,128)S(1)} %subtract_multiply_fusion, f32[256]{0:T(256)S(1)} %copy-done.5), kind=kLoop, calls=%fused_computation | loop fusion | flops 20971520 | bytes 25232384 | tf_op jit(solution)/shard_map/convert_element_type | solution.py:48
  45.5 8.2 %convolution_convert_fusion = bf16[16,256,256]{2,1,0:T(8,128)(2,1)S(1)} fusion(bf16[16,1024,256]{2,1,0:T(8,128)(2,1)} %multiply_convert_fusion, bf16[16,1024,256]{2,1,0:T(8,128)(2,1)} %param.8), kind=kOutput, calls=%fused_computation.19 | convolution fusion | flops 2148532224 | bytes 18874368 | tf_op jit(solution)/shard_map/slo,slc->soc/dot_general | solution.py:49
  53.8 0.0 copy-start
  53.8 0.0 copy-start.7
  53.8 0.0 copy-start.4
  53.8 9.6 %fusion.18 = bf16[16,256,256]{2,1,0:T(8,128)(2,1)} fusion(bf16[16,1024,256]{2,1,0:T(8,128)(2,1)} %param.8, bf16[16,1024,256]{2,1,0:T(8,128)(2,1)} %multiply_convert_fusion), kind=kOutput, calls=%fused_computation.18 | convolution fusion | flops 2114977792 | bytes 18612224 | tf_op jit(solution)/shard_map/slo,slc->soc/dot_general | solution.py:52
  63.4 0.0 copy-done
  63.4 14.6 %all_gather.7 = bf16[512,512]{1,0:T(8,128)(2,1)S(1)} all-gather(bf16[512,128]{1,0:T(8,128)(2,1)S(1)} %copy-done), channel_id=1, replica_groups=mesh['walker'=32,'owner'=4] {'owner'}, dimensions={1}, use_global_device_ids=true | all-gather | bytes 655360 | tf_op jit(solution)/shard_map/all_gather | solution.py:67
  78.1 0.0 copy-done.7
  78.1 0.6 reduce_sum.38
  78.7 0.0 copy-done.4
  78.7 12.0 %all_gather.6 = bf16[256,256]{0,1:T(8,128)(2,1)S(1)} all-gather(bf16[256,64]{0,1:T(8,128)(2,1)S(1)} %copy-done.4), channel_id=1, replica_groups=mesh['walker'=32,'owner'=4] {'owner'}, dimensions={1}, use_global_device_ids=true | all-gather | bytes 163840 | tf_op jit(solution)/shard_map/all_gather | solution.py:19
  90.6 66.1 %psum.21 = f32[]{:T(128)} all-reduce(f32[]{:T(128)} %reduce_sum.38), channel_id=1, replica_groups=mesh['walker'=32,'owner'=4] {'walker','owner'}, use_global_device_ids=true, to_apply=%region_3.0 | all-reduce | flops 1 | bytes 8 | tf_op jit(solution)/shard_map/psum | solution.py:17
  157.4 6.2 %multiply_reduce_fusion.1 = (f32[256,512]{1,0:T(8,128)S(1)}, bf16[16,256,512]{2,1,0:T(8,128)(2,1)}) fusion(bf16[512,512]{1,0:T(8,128)(2,1)S(1)} %all_gather.7, bf16[16,256,256]{2,1,0:T(8,128)(2,1)S(1)} %convolution_convert_fusion, bf16[16,256,256]{2,1,0:T(8,128)(2,1)} %fusion.18, bf16[256,256]{0,1:T(8,128)(2,1)S(1)} %all_gather.6), kind=kOutput, calls=%fused_computation.5 | convolution fusion | flops 3237871616 | bytes 9568256 | tf_op jit(solution)/shard_map/skc,cm->skm/dot_general | solution.py:64
  163.6 4.7 %fusion = f32[1,256,512]{2,0,1:T(1,128)S(1)} fusion(bf16[16,256,512]{2,1,0:T(8,128)(2,1)} %get-tuple-element.5, f32[16]{0:T(128)S(1)} %copy-done.7, f32[]{:T(128)S(6)} %div.29), kind=kOutput, calls=%fused_computation.3 | convolution fusion | flops 4194320 | bytes 4718660 | tf_op jit(solution)/shard_map/s,skm->km/dot_general | solution.py:71
  168.4 1.1 pad_maximum_fusion
  169.5 0.0 all-reduce.3.cloned.1.call-update
  169.5 0.0 reduce-scatter.2.cloned.1.call-start
  169.5 144.0 %all-reduce.3.cloned.1.call-done = f32[2,256,512]{2,1,0:T(8,128)} async-done(((f32[2,256,512]{2,1,0:T(8,128)}), f32[2,256,512]{2,1,0:T(8,128)}) %all-reduce.3.cloned.1.call-update) | async-done | bytes 1048592 | tf_op jit(solution)/shard_map/psum | solution.py:73
  313.5 0.9 fusion.28
  314.4 0.0 copy-start.1
  314.4 2.2 fusion.23
  316.7 0.0 reduce-scatter.2.cloned.1.call-update
  316.7 20.8 %reduce-scatter.2.cloned.1.call-done = f32[256,128]{1,0:T(8,128)} async-done(((f32[256,512]{1,0:T(8,128)}), f32[256,128]{1,0:T(8,128)}) %reduce-scatter.2.cloned.1.call-update) | async-done | bytes 131088 | tf_op jit(solution)/shard_map/reduce_scatter | solution.py:85
  337.5 1.5 multiply_reduce_fusion.2
  339.0 9.0 %psum.23 = f32[]{:T(128)} all-reduce(f32[]{:T(128)} %multiply_reduce_fusion.2), channel_id=1, replica_groups=mesh['walker'=32,'owner'=4] {'owner'}, use_global_device_ids=true, to_apply=%region_7.0 | all-reduce | flops 1 | bytes 8 | tf_op jit(solution)/shard_map/psum | solution.py:86
  348.7 1.6 broadcast_divide_fusion
  350.3 0.0 copy-done.1
  (2 shorter events, 0.1 us)
Async XLA Ops:
  7.2 11.5 %copy-start.2 = (bf16[256,512]{1,0:T(8,128)(2,1)S(1)}, bf16[256,512]{1,0:T(8,128)(2,1)}, u32[]{:S(2)}) copy-start(bf16[256,512]{1,0:T(8,128)(2,1)} %param.10) | copy-start | bytes 786436
  7.2 11.5 %copy-start.6 = (f32[256]{0:T(256)S(1)}, f32[256]{0:T(256)}, u32[]{:S(2)}) copy-start(f32[256]{0:T(256)} %param.11) | copy-start | bytes 3076
  7.2 11.4 %copy-start.5 = (f32[256]{0:T(256)S(1)}, f32[256]{0:T(256)}, u32[]{:S(2)}) copy-start(f32[256]{0:T(256)} %param.12) | copy-start | bytes 3076
  7.2 306.3 %all-reduce.3.cloned.1.call-start = ((), (), s32[]{:S(2)}) async-start(), calls=%async_computation.1 | async-start | bytes 2097152 | tf_op jit(solution)/shard_map/psum | solution.py:73
  18.6 16.8 %copy-start.3 = (s32[16,1024]{1,0:T(8,128)S(1)}, s32[16,1024]{1,0:T(8,128)}, u32[]{:S(2)}) copy-start(s32[16,1024]{1,0:T(8,128)} %param.9) | copy-start | bytes 196612
  53.8 9.6 %copy-start = (bf16[512,128]{1,0:T(8,128)(2,1)S(1)}, bf16[512,128]{1,0:T(8,128)(2,1)}, u32[]{:S(2)}) copy-start(bf16[512,128]{1,0:T(8,128)(2,1)} %param.15) | copy-start | bytes 393220
  53.8 24.3 %copy-start.7 = (f32[16]{0:T(128)S(1)}, f32[16]{0:T(128)}, u32[]{:S(2)}) copy-start(f32[16]{0:T(128)} %param.13) | copy-start | bytes 196
  53.8 24.9 %copy-start.4 = (bf16[256,64]{0,1:T(8,128)(2,1)S(1)}, bf16[256,64]{0,1:T(8,128)(2,1)}, u32[]{:S(2)}) copy-start(bf16[256,64]{0,1:T(8,128)(2,1)} %param.14) | copy-start | bytes 98308
  169.5 168.0 %reduce-scatter.2.cloned.1.call-start = ((), (), s32[]{:S(2)}) async-start(), calls=%async_computation.2 | async-start | bytes 655360 | tf_op jit(solution)/shard_map/reduce_scatter | solution.py:85
  314.4 35.9 %copy-start.1 = (f32[256,128]{1,0:T(8,128)}, f32[256,128]{1,0:T(8,128)S(1)}, u32[]{:S(2)}) copy-start(f32[256,128]{1,0:T(8,128)S(1)} %fusion.28) | copy-start | bytes 393220
Sparse Core Ops, SparseCore 0:
  169.6 143.8 all-reduce.2
  316.8 20.6 reduce-scatter.1
where the time goes:
time: 358 us; the launch traced here: 357 us
  waiting for transfers between devices  165 us (46%)
  blocking collectives  102 us (28%)
  matrix products  59.2 us (17%)
  other arithmetic  15.8 us (4%)
  between operations  15.5 us (4%)
    psum x1, waiting for transfers between devices, body(): totals = lax.psum(stacked, ('walker', 'owner'))  144 us
    psum x1, blocking collectives, body(): energy_total = lax.psum(jnp.sum(energies), ('walker', 'owner'))  66.1 us
    reduce_scatter x1, waiting for transfers between devices, body(): lax.psum_scatter(back_term, 'owner', scatter_dimension=1, tiled=True)  20.8 us
    dot_general x1, matrix products, body(): jnp.einsum('slc,oc->slo', block_input_rows, conv_weight[:, channel_count:...  16.8 us
    all_gather x1, blocking collectives, body(): lax.all_gather(basis_in, 'owner', axis=1, tiled=True)  14.6 us
    all_gather x1, blocking collectives, body(): full_out = lax.all_gather(basis_out, 'owner', axis=1, tiled=True)  12 us
    dot_general x1, matrix products, body(): jnp.einsum('slc,oc->slo', block_input_rows, conv_weight[:, :channel_count...  11.4 us
    convert_element_type x1, other arithmetic, body(): backward_signal = backward_signal.astype(jnp.bfloat16)  10 us
  transfers between devices with their start and end apart: 2, of which 2 were waited for; matrix products, arithmetic and copies ran while one was open for 0% of the time, Pallas kernels for 0%

commit v1 on v0

--- a/solution.py
+++ b/solution.py
@@ -5,6 +5,28 @@
 
 DILATION_STEP = 16
 DAMPING = 0.01
+
+
+def laid_out(tiles, dim):
+    tiles = jnp.moveaxis(tiles, 0, dim)
+    shape = tiles.shape
+    return tiles.reshape(*shape[:dim], shape[dim] * shape[dim + 1], *shape[dim + 2 :])
+
+
+def ring_gather(x, axis, dim):
+    devices = lax.axis_size(axis)
+    pairs = [(i, (i + 1) % devices) for i in range(devices)]
+    back = [(b, a) for a, b in pairs]
+    lower, upper = ([], [])
+    for step in range(devices - 1):
+        if step % 2 == 0:
+            lower.append(lax.ppermute(lower[-1] if lower else x, axis, pairs))
+        else:
+            upper.append(lax.ppermute(upper[-1] if upper else x, axis, back))
+    pieces = jnp.stack([*lower[::-1], x, *upper])
+    shift = lax.axis_index(axis) - len(lower)
+    pieces = pieces[(jnp.arange(devices) - shift) % devices]
+    return laid_out(pieces, dim)
 
 
 def body(
@@ -16,7 +38,7 @@
     total_samples = local_sample_count * lax.axis_size("walker") * lax.axis_size("owner")
     energy_total = lax.psum(jnp.sum(energies), ("walker", "owner"))
     energy_mean = energy_total / total_samples
-    full_out = lax.all_gather(basis_out, "owner", axis=1, tiled=True)
+    full_out = ring_gather(basis_out, "owner", 1)
     now_part = jnp.einsum(
         "slc,oc->slo",
         block_input_rows,

time: 358 us -> 350 us (0.978)
  blocking collectives: 102 us -> 87.9 us
  starting transfers between devices: 0.08 us -> 4.84 us
    all_gather x1 -> x0, blocking collectives: 12 us -> none  [body(): full_out = lax.all_gather(basis_out, 'owner', axis=1, tiled=True)]
    ppermute x0 -> x3, starting transfers between devices: none -> 4.76 us  [the longest x2 3.18 us: ring_gather(): lower.append(lax.ppermute(lower[-1] if lower else x, axis, pairs))]
  transfers between devices with their start and end apart: 2 -> 5, of which waited for: 2 -> 2; matrix products, arithmetic and copies ran while one was open for 0% -> 16% of each run, Pallas kernels for 0% -> 0%
where the time goes in v1:
time: 350 us; the launch traced here: 349 us
  waiting for transfers between devices  165 us (47%)
  blocking collectives  87.9 us (25%)
  matrix products  59.1 us (17%)
  other arithmetic  16.5 us (5%)
  between operations  15.5 us (4%)
  starting transfers between devices  4.84 us (1%)
    psum x1, waiting for transfers between devices, body(): totals = lax.psum(stacked, ('walker', 'owner'))  144 us
    psum x1, blocking collectives, body(): energy_total = lax.psum(jnp.sum(energies), ('walker', 'owner'))  65.6 us
    reduce_scatter x1, waiting for transfers between devices, body(): lax.psum_scatter(back_term, 'owner', scatter_dimension=1, tiled=True)  21 us
    dot_general x1, matrix products, body(): jnp.einsum('slc,oc->slo', block_input_rows, conv_weight[:, channel_count:...  16.8 us
    all_gather x1, blocking collectives, body(): lax.all_gather(basis_in, 'owner', axis=1, tiled=True)  13.4 us
    dot_general x1, matrix products, body(): jnp.einsum('slc,oc->slo', block_input_rows, conv_weight[:, :channel_count...  11.4 us
    convert_element_type x1, other arithmetic, body(): backward_signal = backward_signal.astype(jnp.bfloat16)  10 us
    dot_general x1, matrix products, body(): jnp.einsum('slo,slc->soc', backward_signal[:, DILATION_STEP:], block_inpu...  9.59 us
  transfers between devices with their start and end apart: 5, of which 2 were waited for; matrix products, arithmetic and copies ran while one was open for 16% of the time, Pallas kernels for 0%

profile of v1, /device:TPU:0, one launch (start us, length us, event | category | flops | bytes accessed | tf_op | source)
XLA Modules:
  0.0 349.4 jit_solution(11802975936836693615)
XLA Ops:
  7.2 0.0 all-reduce.3.cloned.1.call-start
  7.2 1.7 collective-permute-start
  8.9 1.6 collective-permute-start.2
  10.5 0.0 copy-start.1
  10.5 0.0 copy-start.4
  10.5 0.0 copy-start.5
  10.5 11.4 %fusion.5 = f32[16,1008,256]{2,1,0:T(8,128)} fusion(bf16[16,1024,256]{2,1,0:T(8,128)(2,1)} %param.8, bf16[256,512]{1,0:T(8,128)(2,1)} %param.10), kind=kOutput, calls=%fused_computation.10 | convolution fusion | flops 2113929216 | bytes 24903680 | tf_op jit(solution)/shard_map/slc,oc->slo/dot_general | solution.py:48
  21.9 0.0 copy-done.1
  21.9 0.0 copy-done.4
  21.9 0.0 copy-done.5
  21.9 0.0 copy-start.2
  21.9 16.8 %multiply_reduce_fusion = (f32[16,1024]{1,0:T(8,128)S(1)}, f32[16,1024,256]{2,1,0:T(8,128)}) fusion(bf16[16,1024,256]{2,1,0:T(8,128)(2,1)} %param.8, f32[256]{0:T(256)S(1)} %copy-done.4, f32[256]{0:T(256)S(1)} %copy-done.5, f32[16,1008,256]{2,1,0:T(8,128)} %fusion.5, bf16[256,512]{1,0:T(8,128)(2,1)S(1)} %copy-done.1), kind=kOutput, calls=%fused_computation.2 | convolution fusion | flops 2172633088 | bytes 50268160 | tf_op jit(solution)/shard_map/slc,oc->slo/dot_general | solution.py:42
  38.7 0.0 copy-done.2
  38.8 10.0 %multiply_convert_fusion = bf16[16,1024,256]{2,1,0:T(8,128)(2,1)} fusion(f32[16,1024,256]{2,1,0:T(8,128)} %get-tuple-element.3, f32[16,1024]{1,0:T(8,128)S(1)} %subtract_multiply_fusion, f32[256]{0:T(256)S(1)} %copy-done.4), kind=kLoop, calls=%fused_computation.1 | loop fusion | flops 20971520 | bytes 25232384 | tf_op jit(solution)/shard_map/convert_element_type | solution.py:70
  48.8 8.2 %convolution_convert_fusion = bf16[16,256,256]{2,1,0:T(8,128)(2,1)S(1)} fusion(bf16[16,1024,256]{2,1,0:T(8,128)(2,1)} %multiply_convert_fusion, bf16[16,1024,256]{2,1,0:T(8,128)(2,1)} %param.8), kind=kOutput, calls=%fused_computation.20 | convolution fusion | flops 2148532224 | bytes 18874368 | tf_op jit(solution)/shard_map/slo,slc->soc/dot_general | solution.py:71
  57.1 0.0 copy-start
  57.1 0.0 copy-start.6
  57.1 0.0 copy-start.3
  57.1 9.6 %fusion.18 = bf16[16,256,256]{2,1,0:T(8,128)(2,1)} fusion(bf16[16,1024,256]{2,1,0:T(8,128)(2,1)} %param.8, bf16[16,1024,256]{2,1,0:T(8,128)(2,1)} %multiply_convert_fusion), kind=kOutput, calls=%fused_computation.19 | convolution fusion | flops 2114977792 | bytes 18612224 | tf_op jit(solution)/shard_map/slo,slc->soc/dot_general | solution.py:74
  66.7 0.0 copy-done
  66.7 13.4 %all_gather.3 = bf16[512,512]{1,0:T(8,128)(2,1)S(1)} all-gather(bf16[512,128]{1,0:T(8,128)(2,1)S(1)} %copy-done), channel_id=1, replica_groups=mesh['walker'=32,'owner'=4] {'owner'}, dimensions={1}, use_global_device_ids=true | all-gather | bytes 655360 | tf_op jit(solution)/shard_map/all_gather | solution.py:89
  80.1 0.0 copy-done.6
  80.1 0.6 reduce_sum.38
  80.7 0.0 collective-permute-done
  80.7 1.5 collective-permute-start.1
  82.2 65.6 %psum.21 = f32[]{:T(128)} all-reduce(f32[]{:T(128)} %reduce_sum.38), channel_id=1, replica_groups=mesh['walker'=32,'owner'=4] {'walker','owner'}, use_global_device_ids=true, to_apply=%region_3.4 | all-reduce | flops 1 | bytes 8 | tf_op jit(solution)/shard_map/psum | solution.py:39
  148.4 0.0 collective-permute-done.2
  148.4 0.0 collective-permute-done.1
  148.4 0.0 copy-done.3
  148.4 0.6 gather_fusion
  149.0 6.2 %multiply_reduce_fusion.1 = (f32[256,512]{1,0:T(8,128)S(1)}, bf16[16,256,512]{2,1,0:T(8,128)(2,1)}) fusion(bf16[512,512]{1,0:T(8,128)(2,1)S(1)} %all_gather.3, bf16[256,256,1]{0,1,2:T(8,128)(2,1)S(1)} %bitcast.46, bf16[16,256,256]{2,1,0:T(8,128)(2,1)S(1)} %convolution_convert_fusion, bf16[16,256,256]{2,1,0:T(8,128)(2,1)} %fusion.18), kind=kOutput, calls=%fused_computation.6 | convolution fusion | flops 3237871616 | bytes 9568256 | tf_op jit(solution)/shard_map/skc,cm->skm/dot_general | solution.py:86
  155.2 4.7 %fusion = f32[1,256,512]{2,0,1:T(1,128)S(1)} fusion(bf16[16,256,512]{2,1,0:T(8,128)(2,1)} %get-tuple-element.5, f32[16]{0:T(128)S(1)} %copy-done.6, f32[]{:T(128)S(6)} %div.28), kind=kOutput, calls=%fused_computation.4 | convolution fusion | flops 4194320 | bytes 4718660 | tf_op jit(solution)/shard_map/s,skm->km/dot_general | solution.py:93
  160.0 1.1 pad_maximum_fusion
  161.1 0.0 all-reduce.3.cloned.1.call-update
  161.1 0.0 reduce-scatter.2.cloned.1.call-start
  161.1 143.9 %all-reduce.3.cloned.1.call-done = f32[2,256,512]{2,1,0:T(8,128)} async-done(((f32[2,256,512]{2,1,0:T(8,128)}), f32[2,256,512]{2,1,0:T(8,128)}) %all-reduce.3.cloned.1.call-update) | async-done | bytes 1048592 | tf_op jit(solution)/shard_map/psum | solution.py:95
  305.0 2.2 fusion.23
  307.2 0.0 reduce-scatter.2.cloned.1.call-update
  307.2 21.0 %reduce-scatter.2.cloned.1.call-done = f32[256,128]{1,0:T(8,128)} async-done(((f32[256,512]{1,0:T(8,128)}), f32[256,128]{1,0:T(8,128)}) %reduce-scatter.2.cloned.1.call-update) | async-done | bytes 131088 | tf_op jit(solution)/shard_map/reduce_scatter | solution.py:107
  328.3 1.5 multiply_reduce_fusion.2
  329.8 1.6 fusion.31
  331.4 8.9 %psum.23 = f32[]{:T(128)} all-reduce(f32[]{:T(128)} %multiply_reduce_fusion.2), channel_id=1, replica_groups=mesh['walker'=32,'owner'=4] {'owner'}, use_global_device_ids=true, to_apply=%region_7.8 | all-reduce | flops 1 | bytes 8 | tf_op jit(solution)/shard_map/psum | solution.py:108
  341.0 1.6 broadcast_divide_fusion
  (5 shorter events, 0.1 us)
Async XLA Ops:
  7.2 297.9 %all-reduce.3.cloned.1.call-start = ((), (), s32[]{:S(2)}) async-start(), calls=%async_computation.1 | async-start | bytes 2097152 | tf_op jit(solution)/shard_map/psum | solution.py:95
  7.2 73.5 %collective-permute-start = (bf16[256,64]{0,1:T(8,128)(2,1)}, bf16[256,64]{0,1:T(8,128)(2,1)S(1)}, u32[]{:S(2)}, u32[]{:S(2)}) collective-permute-start(bf16[256,64]{0,1:T(8,128)(2,1)} %param.14), channel_id=1, source_target_pairs={{0,1},{1,2},{2,3},{3,0},{4,5},{5,6},{6,7},{7,4},{8,9},{9,10},{10,1... | collective-permute-start | bytes 98312 | tf_op jit(solution)/shard_map/ppermute | solution.py:23
  8.9 139.4 %collective-permute-start.2 = (bf16[256,64]{0,1:T(8,128)(2,1)}, bf16[256,64]{0,1:T(8,128)(2,1)S(1)}, u32[]{:S(2)}, u32[]{:S(2)}) collective-permute-start(bf16[256,64]{0,1:T(8,128)(2,1)} %param.14), channel_id=1, source_target_pairs={{1,0},{2,1},{3,2},{0,3},{5,4},{6,5},{7,6},{4,7},{9,8},{10,9},{11,1... | collective-permute-start | bytes 98312 | tf_op jit(solution)/shard_map/ppermute | solution.py:25
  10.5 11.4 %copy-start.1 = (bf16[256,512]{1,0:T(8,128)(2,1)S(1)}, bf16[256,512]{1,0:T(8,128)(2,1)}, u32[]{:S(2)}) copy-start(bf16[256,512]{1,0:T(8,128)(2,1)} %param.10) | copy-start | bytes 786436
  10.5 11.4 %copy-start.4 = (f32[256]{0:T(256)S(1)}, f32[256]{0:T(256)}, u32[]{:S(2)}) copy-start(f32[256]{0:T(256)} %param.12) | copy-start | bytes 3076
  10.5 11.4 %copy-start.5 = (f32[256]{0:T(256)S(1)}, f32[256]{0:T(256)}, u32[]{:S(2)}) copy-start(f32[256]{0:T(256)} %param.11) | copy-start | bytes 3076
  21.9 16.8 %copy-start.2 = (s32[16,1024]{1,0:T(8,128)S(1)}, s32[16,1024]{1,0:T(8,128)}, u32[]{:S(2)}) copy-start(s32[16,1024]{1,0:T(8,128)} %param.9) | copy-start | bytes 196612
  57.1 9.6 %copy-start = (bf16[512,128]{1,0:T(8,128)(2,1)S(1)}, bf16[512,128]{1,0:T(8,128)(2,1)}, u32[]{:S(2)}) copy-start(bf16[512,128]{1,0:T(8,128)(2,1)} %param.15) | copy-start | bytes 393220
  57.1 23.0 %copy-start.6 = (f32[16]{0:T(128)S(1)}, f32[16]{0:T(128)}, u32[]{:S(2)}) copy-start(f32[16]{0:T(128)} %param.13) | copy-start | bytes 196
  57.1 91.3 %copy-start.3 = (bf16[256,64]{0,1:T(8,128)(2,1)S(1)}, bf16[256,64]{0,1:T(8,128)(2,1)}, u32[]{:S(2)}) copy-start(bf16[256,64]{0,1:T(8,128)(2,1)} %param.14) | copy-start | bytes 98308
  80.7 67.7 %collective-permute-start.1 = (bf16[256,64]{0,1:T(8,128)(2,1)S(1)}, bf16[256,64]{0,1:T(8,128)(2,1)S(1)}, u32[]{:S(2)}, u32[]{:S(2)}) collective-permute-start(bf16[256,64]{0,1:T(8,128)(2,1)S(1)} %collective-permute-done), channel_id=1, source_target_pairs={{0,1},{1,2},{2,3},{3,0},{4,5},{5,6},{6,7},{7,4},{8,9},{9,10},{10,1... | collective-permute-start | bytes 98312 | tf_op jit(solution)/shard_map/ppermute | solution.py:23
  161.1 167.2 %reduce-scatter.2.cloned.1.call-start = ((), (), s32[]{:S(2)}) async-start(), calls=%async_computation.2 | async-start | bytes 655360 | tf_op jit(solution)/shard_map/reduce_scatter | solution.py:107
Sparse Core Ops, SparseCore 0:
  161.2 143.7 all-reduce.2
  307.5 20.6 reduce-scatter.1
